TPU v7x, 32 devices: a whole 2x2x4 slice. The times are simulated.
32 devices in a mesh: group: 4 (over x, core), inner: 8 (over z, y).
Axes of the slice: x: 2, y: 2, z: 4, core: 2. Of those that a mesh axis runs over, the one named last changes fastest.
Arguments:
- tokens: bfloat16 [2, 2048, 2048], P(None, ('group', 'inner')), may hold values from -6 to 6
- route_weight: float32 [2, 2048, 6], P(None, ('group', 'inner')), may hold values from 0.05 to 0.5
- routes: int32 [2, 2048, 6], P(None, ('group', 'inner')), may hold values from 0 to 63, all different within a row; in each aligned block of 64 rows (0 to 63, 64 to 127, ..., all dimensions but the last counted through in order) at most 6 rows name the same one
- replica: int32 [2, 2048, 6], P(None, ('group', 'inner')), may hold values from 0 to 1
- old_place: int32 [128], replicated, may hold values from 0 to 63, as said below
- new_src: int32 [128], replicated, may hold values from 0 to 127, as said below
- w_in: bfloat16 [128, 2816, 2048], P(('group', 'inner')), may hold values from -0.125 to 0.125
- w_out: bfloat16 [128, 1408, 2048], P(('group', 'inner')), may hold values from -0.15625 to 0.15625
- queries: bfloat16 [2, 32, 16, 576], P(None, 'group'), may hold values from -21 to 21
- latent_cache: bfloat16 [2, 384, 256, 576], P(None, ('group', 'inner')), may hold values from -6 to 6
- block_req: int32 [2, 384], P(None, ('group', 'inner')), may hold values from 0 to 7, as said below
- block_len: int32 [2, 384], P(None, ('group', 'inner')), may hold values from 0 to 256
Outputs:
- moe_out: bfloat16 [2, 2048, 2048], P(None, ('group', 'inner'))
- attention: bfloat16 [2, 32, 16, 512], P(None, 'group')
Inputs may be any that keep to these rules, and one draw needn't show every extreme that they name: `routes`: within one batch, in each aligned block of 64 tokens (the tokens of one device) no expert is named by more than 6 tokens; a token names 6 different experts. `old_place`: every expert holds exactly two slots. old_place[new_src] names every expert exactly twice. `block_req`: in each batch and group one request has exactly 8192 positions and the others 1024 to 2048; a request's positions fill whole blocks except its last; blocks with block_len 0 are unused.
All inputs are finite; a program needn't handle non-finite values.
Results may differ from a plain program's by a relative error of at most 0.014.
Values may be sent and summed in bfloat16 or wider, within the bound.
A program may use at most 256 MiB of HBM per device.

v0:
```python
from functools import partial

import jax
import jax.numpy as jnp
from jax import lax
from jax.sharding import PartitionSpec as P

FF = 1408
EXPERTS = 64
TOPK = 6
LAT = 512
MOST = 6


score_scale = 192.0 ** (-0.5)
floor_value = -1e30


def joined(shard, axis, join):
    gathered = jax.tree.map(
        lambda a, kind: lax.all_gather(a.astype(kind), axis),
        shard,
        (jnp.bfloat16, jnp.bfloat16, jnp.bfloat16),
    )

    def take(source):
        return jax.tree.map(
            lambda a, own: lax.dynamic_index_in_dim(a, source, 0, False).astype(own.dtype),
            gathered,
            shard,
        )

    return lax.fori_loop(
        1, lax.axis_size(axis), lambda source, state: join(state, take(source)), take(0)
    )


def block_attention(queries, latent_cache, block_req, block_len, latent):
    requests, head_count, feat_width = queries.shape
    blocks, cache_rows, _ = latent_cache.shape
    belongs = block_req[:, None] == jnp.arange(requests, dtype=jnp.int32)[None, :]
    chosen = jnp.dot(
        belongs.astype(jnp.bfloat16),
        queries.reshape(requests, head_count * feat_width),
        preferred_element_type=jnp.float32,
    )
    chosen = chosen.astype(jnp.bfloat16).reshape(blocks, head_count, feat_width)
    scores = (
        jnp.einsum("chk,cpk->chp", chosen, latent_cache, preferred_element_type=jnp.float32)
        * score_scale
    )
    live_rows = jnp.arange(cache_rows, dtype=jnp.int32)[None, :] < block_len[:, None]
    scores = jnp.where(live_rows[:, None, :], scores, floor_value)
    block_max = jnp.max(scores, axis=2)
    req_max = jnp.max(jnp.where(belongs[:, :, None], block_max[:, None, :], floor_value), axis=0)
    own_max = jnp.sum(jnp.where(belongs[:, :, None], req_max[None, :, :], 0.0), axis=1)
    exp_scores = jnp.where(live_rows[:, None, :], jnp.exp(scores - own_max[:, :, None]), 0.0)
    block_total = jnp.sum(exp_scores, axis=2)
    weights = exp_scores.astype(jnp.bfloat16)
    block_out = jnp.einsum(
        "chp,cpl->chl", weights, latent_cache[:, :, :latent], preferred_element_type=jnp.float32
    )
    belongs_f = belongs.astype(jnp.float32)
    req_total = jnp.einsum("cr,ch->rh", belongs_f, block_total, precision=lax.Precision.HIGHEST)
    req_out = jnp.einsum("cr,chl->rhl", belongs_f, block_out, precision=lax.Precision.HIGHEST)
    return (req_max, req_total, req_out)


def merge_parts(part_one, part_two):
    max_one, total_one, out_one = part_one
    max_two, total_two, out_two = part_two
    joint_max = jnp.maximum(max_one, max_two)
    scale_one = jnp.exp(max_one - joint_max)
    scale_two = jnp.exp(max_two - joint_max)
    joint_total = total_one * scale_one + total_two * scale_two
    joint_out = out_one * scale_one[..., None] + out_two * scale_two[..., None]
    return (joint_max, joint_total, joint_out)


def slot_of_route(expert_of_slot, routes, replica):
    slot_count = expert_of_slot.shape[0]
    slot_hits = (expert_of_slot[:, None] == jnp.arange(EXPERTS, dtype=jnp.int32)[None, :]).astype(
        jnp.int32
    )
    replica_rank = jnp.sum((jnp.cumsum(slot_hits, axis=0) - slot_hits) * slot_hits, axis=1)
    flat_expert = routes.reshape(-1)
    flat_replica = replica.reshape(-1)
    matches = (expert_of_slot[None, :] == flat_expert[:, None]) & (
        replica_rank[None, :] == flat_replica[:, None]
    )
    return jnp.sum(jnp.where(matches, jnp.arange(slot_count, dtype=jnp.int32)[None, :], 0), axis=1)


def table_lookup(indices, lookup_table):
    matches = indices[:, None] == jnp.arange(lookup_table.shape[0], dtype=jnp.int32)[None, :]
    return jnp.sum(jnp.where(matches, lookup_table[None, :], 0), axis=1)


def expert_block(arrived, w_in, w_out):
    gate_up = jnp.einsum("nsmd,sfd->nsmf", arrived, w_in, preferred_element_type=jnp.float32)
    hidden = (jax.nn.silu(gate_up[..., :FF]) * gate_up[..., FF:]).astype(jnp.bfloat16)
    return jnp.einsum("nsmf,sfd->nsmd", hidden, w_out, preferred_element_type=jnp.float32).astype(
        jnp.bfloat16
    )


def moe_batch(tokens, route_weight, target, w_in, w_out, n_group, n_inner):
    slot_count = 2 * EXPERTS
    devices = n_group * n_inner
    slot_dev = slot_count // devices
    tok_count, feat_width = tokens.shape
    slot_hits = (target[:, None] == jnp.arange(slot_count, dtype=jnp.int32)[None, :]).astype(
        jnp.int32
    )
    position = jnp.sum((jnp.cumsum(slot_hits, axis=0) - slot_hits) * slot_hits, axis=1)
    box_row = (target * MOST + position).reshape(tok_count, TOPK)
    box_hits = box_row[:, :, None] == jnp.arange(slot_count * MOST, dtype=jnp.int32)[None, None, :]
    send_table = jnp.sum(box_hits.astype(jnp.float32), axis=1).astype(jnp.bfloat16)
    back_table = jnp.sum(jnp.where(box_hits, route_weight[:, :, None], 0.0), axis=1)
    outbox = jnp.einsum("nr,nd->rd", send_table, tokens, preferred_element_type=jnp.float32).astype(
        jnp.bfloat16
    )
    outbox = outbox.reshape(slot_count, MOST, feat_width)
    arrived = lax.all_to_all(
        outbox.reshape(devices, slot_dev, MOST, feat_width),
        ("group", "inner"),
        split_axis=0,
        concat_axis=0,
        tiled=True,
    )
    served = expert_block(arrived, w_in, w_out)
    returned = lax.all_to_all(served, ("group", "inner"), split_axis=0, concat_axis=0, tiled=True)
    flat_rows = returned.reshape(slot_count * MOST, feat_width)
    combined = jnp.dot(back_table, flat_rows.astype(jnp.float32), precision=lax.Precision.HIGHEST)
    return combined.astype(jnp.bfloat16)


def local(
    tokens,
    route_weight,
    routes,
    replica,
    old_place,
    new_src,
    w_in,
    w_out,
    queries,
    latent_cache,
    block_req,
    block_len,
):
    n_group = lax.axis_size("group")
    n_inner = lax.axis_size("inner")
    slot_first = slot_of_route(old_place, routes[0], replica[0])
    batch_one = moe_batch(tokens[0], route_weight[0], slot_first, w_in, w_out, n_group, n_inner)
    new_expert = table_lookup(new_src, old_place)
    slot_second = slot_of_route(new_expert, routes[1], replica[1])
    second_target = table_lookup(slot_second, new_src)
    batch_two = moe_batch(tokens[1], route_weight[1], second_target, w_in, w_out, n_group, n_inner)
    moe_out = jnp.stack([batch_one, batch_two])
    attend = jax.vmap(partial(block_attention, latent=LAT))
    req_max, req_total, req_out = attend(queries, latent_cache, block_req, block_len)
    req_max, req_total, req_out = joined((req_max, req_total, req_out), "inner", merge_parts)
    attention = (req_out / req_total[..., None]).astype(jnp.bfloat16)
    return (moe_out, attention)


def solution(mesh):
    in_specs = (
        P(None, ("group", "inner"), None),
        P(None, ("group", "inner"), None),
        P(None, ("group", "inner"), None),
        P(None, ("group", "inner"), None),
        P(),
        P(),
        P(("group", "inner"), None, None),
        P(("group", "inner"), None, None),
        P(None, "group", None, None),
        P(None, ("group", "inner"), None, None),
        P(None, ("group", "inner")),
        P(None, ("group", "inner")),
    )
    out_specs = (P(None, ("group", "inner"), None), P(None, "group", None, None))
    return jax.shard_map(local, mesh=mesh, in_specs=in_specs, out_specs=out_specs, check_vma=False)
```

profile of v0, /device:TPU:0, one launch (start us, length us, event | category | flops | bytes accessed | tf_op | source)
XLA Modules:
  0.0 465.6 jit_solution(13361185022250409848)
XLA Ops:
  8.5 1.4 fusion.77
  10.1 1.4 fusion.76
  16.1 1.9 convolution_convert_fusion.1
  18.0 2.9 reshape_reshape.7
  20.9 6.9 %copy.106 = bf16[32,4,6,2048]{3,1,2,0:T(4,128)(2,1)} copy(bf16[32,4,6,2048]{3,2,1,0:T(8,128)(2,1)} %reshape_reshape.7) | data formatting | bytes 6291456 | tf_op jit(solution)/shard_map/reshape;reshape | solution.py:125
  27.7 7.3 %all-to-all-start.2 = ((bf16[32,4,6,2048]{3,1,2,0:T(4,128)(2,1)}), bf16[32,4,6,2048]{3,1,2,0:T(4,128)(2,1)S(1)}, u32[]{:S(2)}, u32[]{:S(2)}) async-start(bf16[32,4,6,2048]{3,1,2,0:T(4,128)(2,1)} %copy.106), calls=%async_computation.2 | async-start | bytes 6291456 | tf_op jit(solution)/shard_map/all_to_all | solution.py:124
  35.3 1.3 reshape.127
  36.5 1.2 convolution_convert_fusion
  37.7 2.3 reshape.150
  40.2 4.4 fusion.78
  45.5 4.5 fusion.11
  51.8 1.4 fusion.66
  53.1 1.6 reduce_window_sum.42
  54.8 1.4 copy.91
  56.1 1.5 eq.199
  57.6 1.4 copy.90
  59.0 1.5 eq.192
  61.5 1.5 select_reduce_fusion.4
  63.0 1.4 copy.92
  66.8 1.3 reduce-window.15
  70.0 1.3 multiply_add_fusion.1
  71.2 1.4 add.88
  72.6 1.4 copy.94
  74.1 1.7 convert_reduce_fusion.1
  75.7 3.7 convolution_convert_fusion.2
  79.4 6.3 %reshape_reshape.6 = bf16[32,4,6,2048]{3,2,1,0:T(8,128)(2,1)} reshape(bf16[768,2048]{1,0:T(8,128)(2,1)} %convolution_convert_fusion.2) | data formatting | bytes 6291456 | tf_op jit(solution)/shard_map/reshape;reshape | solution.py:125
  85.6 6.9 %copy.96 = bf16[32,4,6,2048]{3,1,2,0:T(4,128)(2,1)} copy(bf16[32,4,6,2048]{3,2,1,0:T(8,128)(2,1)} %reshape_reshape.6) | data formatting | bytes 6291456 | tf_op jit(solution)/shard_map/reshape;reshape | solution.py:125
  92.5 40.9 %all-to-all-done.2 = bf16[32,4,6,2048]{3,1,2,0:T(4,128)(2,1)S(1)} async-done(((bf16[32,4,6,2048]{3,1,2,0:T(4,128)(2,1)}), bf16[32,4,6,2048]{3,1,2,0:T(4,128)(2,1)S(1)}, u32[]{:S(2)}, u32[]{:S(2)}) %all-to-all-start.2) | async-done | bytes 3145760 | tf_op jit(solution)/shard_map/all_to_all | solution.py:124
  133.4 3.7 all-to-all-start
  137.1 24.7 %fusion.16 = f32[32,4,6,2816]{3,0,2,1:T(8,128)} fusion(bf16[4,2816,2048]{2,1,0:T(8,128)(2,1)} %param.20, bf16[32,4,6,2048]{3,1,2,0:T(4,128)(2,1)S(1)} %all-to-all-done.2), kind=kOutput, calls=%fused_computation.20 | convolution fusion | flops 8858370048 | bytes 57933824 | tf_op jit(solution)/shard_map/nsmd,sfd->nsmf/dot_general | solution.py:100
  161.8 15.3 %fusion.29 = bf16[32,4,6,2048]{3,0,2,1:T(8,128)(2,1)S(1)} fusion(bf16[4,1408,2048]{2,1,0:T(8,128)(2,1)} %param.21, f32[32,4,6,2816]{3,0,2,1:T(8,128)} %fusion.16), kind=kOutput, calls=%fused_computation.31 | convolution fusion | flops 4437245952 | bytes 34865152 | tf_op jit(solution)/shard_map/nsmf,sfd->nsmd/dot_general | solution.py:102
  177.2 4.1 copy.108
  181.3 28.8 %all-to-all-done = bf16[32,4,6,2048]{3,1,2,0:T(4,128)(2,1)} async-done(((bf16[32,4,6,2048]{3,1,2,0:T(4,128)(2,1)}), bf16[32,4,6,2048]{3,1,2,0:T(4,128)(2,1)}, u32[]{:S(2)}, u32[]{:S(2)}) %all-to-all-start) | async-done | bytes 3145760 | tf_op jit(solution)/shard_map/all_to_all | solution.py:124
  210.1 3.2 all-to-all-start.3
  213.3 24.6 %fusion.13 = f32[32,4,6,2816]{3,0,2,1:T(8,128)} fusion(bf16[4,2816,2048]{2,1,0:T(8,128)(2,1)} %param.20, bf16[32,4,6,2048]{3,1,2,0:T(4,128)(2,1)} %all-to-all-done), kind=kOutput, calls=%fused_computation.19 | convolution fusion | flops 8858370048 | bytes 57933824 | tf_op jit(solution)/shard_map/nsmd,sfd->nsmf/dot_general | solution.py:100
  237.9 17.1 %fusion.32 = bf16[32,4,6,2048]{3,0,2,1:T(8,128)(2,1)} fusion(bf16[4,1408,2048]{2,1,0:T(8,128)(2,1)} %param.21, f32[32,4,6,2816]{3,0,2,1:T(8,128)} %fusion.13), kind=kOutput, calls=%fused_computation.32 | convolution fusion | flops 4437245952 | bytes 34865152 | tf_op jit(solution)/shard_map/nsmf,sfd->nsmd/dot_general | solution.py:102
  255.0 6.0 %copy.98 = bf16[32,4,6,2048]{3,1,2,0:T(4,128)(2,1)} copy(bf16[32,4,6,2048]{3,0,2,1:T(8,128)(2,1)} %fusion.32) | data formatting | bytes 6291456 | tf_op jit(solution)/shard_map/convert_element_type | solution.py:102
  261.0 25.3 %all-to-all-done.3 = bf16[32,4,6,2048]{3,1,2,0:T(4,128)(2,1)S(1)} async-done(((bf16[32,4,6,2048]{3,1,2,0:T(4,128)(2,1)}), bf16[32,4,6,2048]{3,1,2,0:T(4,128)(2,1)S(1)}, u32[]{:S(2)}, u32[]{:S(2)}) %all-to-all-start.3) | async-done | bytes 3145760 | tf_op jit(solution)/shard_map/all_to_all | solution.py:132
  286.3 3.6 all-to-all-start.1
  290.7 90.9 %all-gather = bf16[16,8,16]{2,1,0:T(8,128)(2,1)S(1)} all-gather(bf16[2,8,16]{2,1,0:T(8,128)(2,1)S(1)} %convert_element_type.172), channel_id=2, replica_groups=mesh['group'=4,'inner'=8] {'inner'}, dimensions={0}, use_global_device_ids=true | all-gather | bytes 4608 | tf_op jit(solution)/shard_map/all_gather | solution.py:21
  383.3 30.6 %all-gather.1 = bf16[16,8,16]{2,1,0:T(8,128)(2,1)S(1)} all-gather(bf16[2,8,16]{2,1,0:T(8,128)(2,1)S(1)} %convolution_convert_fusion.6), channel_id=3, replica_groups=mesh['group'=4,'inner'=8] {'inner'}, dimensions={0}, use_global_device_ids=true | all-gather | bytes 4608 | tf_op jit(solution)/shard_map/all_gather | solution.py:21
  414.9 13.0 %while.19 = (s32[]{:T(128)}, f32[2,8,16]{2,1,0:T(8,128)S(1)}, f32[2,8,16]{2,1,0:T(8,128)S(1)}, f32[2,8,16,512]{3,2,1,0:T(8,128)S(1)}, bf16[8,2,8,16]{3,2,1,0:T(8...) while((s32[]{:T(128)}, f32[2,8,16]{2,1,0:T(8,128)S(1)}, ...), condition=%wide.region_23.24_spmd, body=%wide.region_22.23_spmd.sunk | while | flops 526341 | bytes 1320087 | solution.py:33
  428.7 6.2 %copy.109 = bf16[32,4,6,2048]{3,2,1,0:T(8,128)(2,1)} copy(bf16[32,4,6,2048]{3,1,2,0:T(4,128)(2,1)} %copy-done) | data formatting | bytes 6291456 | tf_op jit(solution)/shard_map/all_to_all | solution.py:132
  434.9 4.9 %reshape.126 = bf16[768,2048]{1,0:T(8,128)(2,1)S(1)} reshape(bf16[32,4,6,2048]{3,2,1,0:T(8,128)(2,1)} %copy.109) | data formatting | bytes 6291456 | tf_op jit(solution)/shard_map/reshape | solution.py:133
  439.8 6.2 %copy.99 = bf16[32,4,6,2048]{3,2,1,0:T(8,128)(2,1)} copy(bf16[32,4,6,2048]{3,1,2,0:T(4,128)(2,1)} %all-to-all-done.1) | data formatting | bytes 6291456 | tf_op jit(solution)/shard_map/all_to_all | solution.py:132
  446.0 6.4 %reshape.124 = bf16[768,2048]{1,0:T(8,128)(2,1)} reshape(bf16[32,4,6,2048]{3,2,1,0:T(8,128)(2,1)} %copy.99) | data formatting | bytes 6291456 | tf_op jit(solution)/shard_map/reshape | solution.py:133
  452.4 1.8 fusion.36
  454.1 3.6 fusion.35
  (84 shorter events, 32.3 us)
Async XLA Ops:
  27.7 8.8 %copy-start.8 = (s32[2,12]{1,0:T(2,128)S(1)}, s32[2,12]{1,0:T(2,128)}, u32[]{:S(2)}) copy-start(s32[2,12]{1,0:T(2,128)} %param.24) | copy-start | bytes 292
  27.7 12.4 %copy-start.10 = (s32[2,12]{1,0:T(2,128)S(1)}, s32[2,12]{1,0:T(2,128)}, u32[]{:S(2)}) copy-start(s32[2,12]{1,0:T(2,128)} %param.25) | copy-start | bytes 292
  27.7 105.7 %all-to-all-start.2 = ((bf16[32,4,6,2048]{3,1,2,0:T(4,128)(2,1)}), bf16[32,4,6,2048]{3,1,2,0:T(4,128)(2,1)S(1)}, u32[]{:S(2)}, u32[]{:S(2)}) async-start(bf16[32,4,6,2048]{3,1,2,0:T(4,128)(2,1)} %copy.106), calls=%async_computation.2 | async-start | bytes 6291456 | tf_op jit(solution)/shard_map/all_to_all | solution.py:124
  35.0 378.9 %all-gather.5.cloned.1.call-start = ((), (), s32[]{:S(2)}) async-start(), calls=%async_computation.4 | async-start | bytes 2359296 | tf_op jit(solution)/shard_map/all_gather | solution.py:21
  40.1 4.5 copy-start.7
  40.2 9.8 %copy-start.4 = (pred[2,12,256]{2,1,0:T(8,128)(4,1)}, pred[2,12,256]{2,1,0:T(8,128)(4,1)S(1)}, u32[]{:S(2)}) copy-start(pred[2,12,256]{2,1,0:T(8,128)(4,1)S(1)} %iota_compare_fusion.12) | copy-start | bytes 18436
  44.6 5.5 %copy-start.9 = (s32[2,12]{1,0:T(2,128)S(1)}, s32[2,12]{1,0:T(2,128)}, u32[]{:S(2)}) copy-start(s32[2,12]{1,0:T(2,128)} %param.24) | copy-start | bytes 292
  44.7 0.8 copy-start.6
  65.5 0.7 copy-start.1
  133.4 76.7 %all-to-all-start = ((bf16[32,4,6,2048]{3,1,2,0:T(4,128)(2,1)}), bf16[32,4,6,2048]{3,1,2,0:T(4,128)(2,1)}, u32[]{:S(2)}, u32[]{:S(2)}) async-start(bf16[32,4,6,2048]{3,1,2,0:T(4,128)(2,1)} %copy.96), calls=%async_computation | async-start | bytes 6291456 | tf_op jit(solution)/shard_map/all_to_all | solution.py:124
  210.1 76.2 %all-to-all-start.3 = ((bf16[32,4,6,2048]{3,1,2,0:T(4,128)(2,1)}), bf16[32,4,6,2048]{3,1,2,0:T(4,128)(2,1)S(1)}, u32[]{:S(2)}, u32[]{:S(2)}) async-start(bf16[32,4,6,2048]{3,1,2,0:T(4,128)(2,1)} %copy.108), calls=%async_computation.3 | async-start | bytes 6291456 | tf_op jit(solution)/shard_map/all_to_all | solution.py:132
  286.3 127.6 %copy-start = (bf16[32,4,6,2048]{3,1,2,0:T(4,128)(2,1)}, bf16[32,4,6,2048]{3,1,2,0:T(4,128)(2,1)S(1)}, u32[]{:S(2)}) copy-start(bf16[32,4,6,2048]{3,1,2,0:T(4,128)(2,1)S(1)} %all-to-all-done.3) | copy-start | bytes 9437188
  286.3 153.5 %all-to-all-start.1 = ((bf16[32,4,6,2048]{3,1,2,0:T(4,128)(2,1)}), bf16[32,4,6,2048]{3,1,2,0:T(4,128)(2,1)}, u32[]{:S(2)}, u32[]{:S(2)}) async-start(bf16[32,4,6,2048]{3,1,2,0:T(4,128)(2,1)} %copy.98), calls=%async_computation.1 | async-start | bytes 6291456 | tf_op jit(solution)/shard_map/all_to_all | solution.py:132
  381.5 32.3 %copy-start.5 = (bf16[16,8,16]{2,1,0:T(8,128)(2,1)}, bf16[16,8,16]{2,1,0:T(8,128)(2,1)S(1)}, u32[]{:S(2)}) copy-start(bf16[16,8,16]{2,1,0:T(8,128)(2,1)S(1)} %all-gather) | copy-start | bytes 12292
  446.0 6.4 %copy-start.2 = (f32[64,768]{1,0:T(8,128)S(1)}, f32[64,768]{1,0:T(8,128)}, u32[]{:S(2)}) copy-start(f32[64,768]{1,0:T(8,128)} %get-tuple-element.198) | copy-start | bytes 589828
  446.0 8.1 %copy-start.3 = (f32[64,768]{1,0:T(8,128)S(1)}, f32[64,768]{1,0:T(8,128)}, u32[]{:S(2)}) copy-start(f32[64,768]{1,0:T(8,128)} %get-tuple-element.196) | copy-start | bytes 589828
Sparse Core Ops, SparseCore 0:
  51.9 73.6 all-gather.4
where the time goes:
time: 473 us; the launch traced here: 466 us
  blocking collectives  121 us (26%)
  matrix products  104 us (22%)
  waiting for transfers between devices  95 us (20%)
  local copies, waits for them, and re-layouts  77.2 us (16%)
  other arithmetic  34.6 us (7%)
  starting transfers between devices  18.1 us (4%)
  between operations  14.5 us (3%)
    all_gather x2, blocking collectives, joined(): lax.all_gather(a.astype(kind), axis)  121 us
    all_to_all x2, waiting for transfers between devices, moe_batch(): lax.all_to_all(outbox.reshape(devices, slot_dev, MOST, feat_width), ('gro...  69.7 us
    dot_general x2, matrix products, expert_block(): jnp.einsum('nsmd,sfd->nsmf', arrived, w_in, preferred_element_type=jnp.fl...  49.3 us
    dot_general x2, matrix products, expert_block(): jnp.einsum('nsmf,sfd->nsmd', hidden, w_out, preferred_element_type=jnp.fl...  32.4 us
    all_to_all x2, waiting for transfers between devices, moe_batch(): lax.all_to_all(served, ('group', 'inner'), split_axis=0, concat_axis=0, t...  25.3 us
    another operation x4, local copies, waits for them, and re-layouts, moe_batch(): outbox.reshape(devices, slot_dev, MOST, feat_width)  22.9 us
    all_to_all x2, local copies, waits for them, and re-layouts, moe_batch(): lax.all_to_all(served, ('group', 'inner'), split_axis=0, concat_axis=0, t...  12.3 us
    reshape x2, local copies, waits for them, and re-layouts, moe_batch(): flat_rows = returned.reshape(slot_count * MOST, feat_width)  11.3 us
  transfers between devices with their start and end apart: 5, of which 3 were waited for; matrix products, arithmetic and copies ran while one was open for 38% of the time, Pallas kernels for 0%

commit v1 on v0

v1 whole, which is shorter than its diff:
```python
from functools import partial

import jax
import jax.numpy as jnp
from jax import lax
from jax.experimental import pallas as pl
from jax.experimental.pallas import tpu as pltpu
from jax.sharding import PartitionSpec as P

MESH = pl.DeviceIdType.MESH
FF = 1408
EXPERTS = 64
TOPK = 6
LAT = 512
MOST = 6
CHUNKS = 4


score_scale = 192.0 ** (-0.5)
floor_value = -1e30


def block_attention(queries, latent_cache, block_req, block_len, latent):
    requests, head_count, feat_width = queries.shape
    blocks, cache_rows, _ = latent_cache.shape
    belongs = block_req[:, None] == jnp.arange(requests, dtype=jnp.int32)[None, :]
    chosen = jnp.dot(
        belongs.astype(jnp.bfloat16),
        queries.reshape(requests, head_count * feat_width),
        preferred_element_type=jnp.float32,
    )
    chosen = chosen.astype(jnp.bfloat16).reshape(blocks, head_count, feat_width)
    scores = (
        jnp.einsum("chk,cpk->chp", chosen, latent_cache, preferred_element_type=jnp.float32)
        * score_scale
    )
    live_rows = jnp.arange(cache_rows, dtype=jnp.int32)[None, :] < block_len[:, None]
    scores = jnp.where(live_rows[:, None, :], scores, floor_value)
    block_max = jnp.max(scores, axis=2)
    req_max = jnp.max(jnp.where(belongs[:, :, None], block_max[:, None, :], floor_value), axis=0)
    own_max = jnp.sum(jnp.where(belongs[:, :, None], req_max[None, :, :], 0.0), axis=1)
    exp_scores = jnp.where(live_rows[:, None, :], jnp.exp(scores - own_max[:, :, None]), 0.0)
    block_total = jnp.sum(exp_scores, axis=2)
    weights = exp_scores.astype(jnp.bfloat16)
    block_out = jnp.einsum(
        "chp,cpl->chl", weights, latent_cache[:, :, :latent], preferred_element_type=jnp.float32
    )
    belongs_f = belongs.astype(jnp.float32)
    req_total = jnp.einsum("cr,ch->rh", belongs_f, block_total, precision=lax.Precision.HIGHEST)
    req_out = jnp.einsum("cr,chl->rhl", belongs_f, block_out, precision=lax.Precision.HIGHEST)
    return (req_max, req_total, req_out)


def join_attention(req_max, req_total, req_out, axis):
    n = lax.axis_size(axis)
    batches, requests, heads, latent = req_out.shape
    share = batches * requests * heads // n
    stats = jnp.stack([req_max.reshape(n, share), req_total.reshape(n, share)], axis=1)
    parts = req_out.astype(jnp.bfloat16).reshape(n, share, latent)
    stats = lax.all_to_all(stats, axis, split_axis=0, concat_axis=0, tiled=True)
    parts = lax.all_to_all(parts, axis, split_axis=0, concat_axis=0, tiled=True)
    joint = jnp.max(stats[:, 0], axis=0)
    scale = jnp.exp(stats[:, 0] - joint[None])
    total = jnp.sum(stats[:, 1] * scale, axis=0)
    summed = jnp.sum(parts.astype(jnp.float32) * scale[..., None], axis=0)
    own = (summed / total[:, None]).astype(jnp.bfloat16)
    whole = lax.all_gather(own, axis, axis=0, tiled=True)
    return whole.reshape(batches, requests, heads, latent)


def replica_keys(expert_of_slot):
    slots = expert_of_slot.shape[0]
    index = jnp.arange(slots, dtype=jnp.int32)
    earlier = (expert_of_slot[None, :] == expert_of_slot[:, None]) & (index[None, :] < index[:, None])
    return expert_of_slot * 2 + jnp.sum(earlier.astype(jnp.int32), axis=1)


def table_lookup(indices, lookup_table):
    matches = indices[:, None] == jnp.arange(lookup_table.shape[0], dtype=jnp.int32)[None, :]
    return jnp.sum(jnp.where(matches, lookup_table[None, :], 0), axis=1)


def places(depth, n_inner):
    width = n_inner // depth
    g, i = lax.axis_index("group"), lax.axis_index("inner")
    z, y = i // width, lax.rem(i, width)
    line = lambda p: (g, p * width + y)
    plane = lambda p: (p // width, z * width + lax.rem(p, width))
    return z, g * width + y, line, plane


def greet(partners):
    barrier = pltpu.get_barrier_semaphore()
    for device in partners:
        pl.semaphore_signal(barrier, inc=1, device_id=device, device_id_type=MESH)
    pl.semaphore_wait(barrier, len(partners))


def remote(src, dst, send, recv, device):
    return pltpu.make_async_remote_copy(
        src_ref=src, dst_ref=dst, send_sem=send, recv_sem=recv, device_id=device, device_id_type=MESH
    )


def dispatch_kernel(depth, n_inner, planes, tok, row, out, gat, tab, box, zs, zr, ps, pr, ls):
    z, me, line, plane = places(depth, n_inner)
    line_to = [lax.rem(z + k, depth) for k in range(1, depth)]
    plane_to = [lax.rem(me + k, planes) for k in range(1, planes)]
    greet([line(p) for p in line_to] + [plane(p) for p in plane_to])
    chunk = gat.shape[3]
    per_box = tab.shape[0] // planes
    flights = []
    for c in range(CHUNKS):
        flight = []
        for k, p in enumerate(line_to):
            copy = remote(
                tok.at[:, pl.ds(c * chunk, chunk)], gat.at[c, z], zs.at[c, k], zr.at[c, k], line(p)
            )
            copy.start()
            flight.append(copy)
        flights.append(flight)
    for c in range(CHUNKS):
        gat[c, z] = tok[:, c * chunk : (c + 1) * chunk]
    step = 256

    def fill(t, carry):
        rows = lax.broadcasted_iota(jnp.int32, (step, tab.shape[1]), 0) + t * step
        total = jnp.zeros((step, tab.shape[1]), jnp.float32)
        for k in range(TOPK):
            total = total + jnp.where(rows == row[k : k + 1, :], 1.0, 0.0)
        tab[pl.ds(pl.multiple_of(t * step, step), step), :] = total.astype(jnp.bfloat16)
        return carry

    lax.fori_loop(0, tab.shape[0] // step, fill, 0)
    sends = []
    for c in range(CHUNKS):
        for copy in flights[c]:
            copy.wait_recv()
        held = gat[c].reshape(tab.shape[1], chunk)

        def build(p, carry):
            table = tab[pl.ds(pl.multiple_of(p * per_box, 16), per_box), :]
            made = jnp.dot(table, held, preferred_element_type=jnp.float32).astype(jnp.bfloat16)
            box[c, p] = made.reshape(box.shape[2:])
            return carry

        lax.fori_loop(0, planes, build, 0)
        for k, p in enumerate(plane_to):
            copy = remote(box.at[c, p], out.at[c, :, me], ps.at[c, k], pr.at[c, k], plane(p))
            copy.start()
            sends.append(copy)
        own = pltpu.make_async_copy(box.at[c, me], out.at[c, :, me], ls.at[c])
        own.start()
        sends.append(own)
    for flight in flights:
        for copy in flight:
            copy.wait_send()
    for copy in sends:
        copy.wait()


def return_kernel(
    depth, n_inner, planes, served, row, weight, out, got, high, low, part, pbuf, own, back, ps, pr, ls, zs, zr
):
    z, me, line, plane = places(depth, n_inner)
    line_to = [lax.rem(z + k, depth) for k in range(1, depth)]
    plane_to = [lax.rem(me + k, planes) for k in range(1, planes)]
    greet([line(p) for p in line_to] + [plane(p) for p in plane_to])
    chunk = got.shape[-1]
    flights = []
    for c in range(CHUNKS):
        flight = []
        for k, p in enumerate(plane_to):
            copy = remote(served.at[c, :, p], got.at[c, me], ps.at[c, k], pr.at[c, k], plane(p))
            copy.start()
            flight.append(copy)
        kept = pltpu.make_async_copy(served.at[c, :, me], got.at[c, me], ls.at[c])
        kept.start()
        flight.append(kept)
        flights.append(flight)
    tokens, rows = high.shape
    step = 256
    for t in range(rows // step):
        cols = lax.broadcasted_iota(jnp.int32, (tokens, step), 1) + t * step
        total = jnp.zeros((tokens, step), jnp.float32)
        for k in range(TOPK):
            total = total + jnp.where(cols == row[:, k : k + 1], weight[:, k : k + 1], 0.0)
        upper = total.astype(jnp.bfloat16)
        high[:, t * step : (t + 1) * step] = upper
        low[:, t * step : (t + 1) * step] = (total - upper.astype(jnp.float32)).astype(jnp.bfloat16)
    sends = []
    for c in range(CHUNKS):
        for copy in flights[c]:
            copy.wait()
        held = got[c].reshape(rows, chunk)
        made = jnp.dot(high[...], held, preferred_element_type=jnp.float32)
        made = made + jnp.dot(low[...], held, preferred_element_type=jnp.float32)
        part[...] = made.reshape(part.shape)
        pbuf[c] = part[...].astype(jnp.bfloat16)
        own[c] = part[z]
        flight = []
        for k, p in enumerate(line_to):
            copy = remote(pbuf.at[c, p], back.at[c, z], zs.at[c, k], zr.at[c, k], line(p))
            copy.start()
            flight.append(copy)
        sends.append(flight)
    for c in range(CHUNKS):
        for copy in sends[c]:
            copy.wait()
        total = own[c]
        for p in line_to:
            total = total + back[c, p].astype(jnp.float32)
        out[:, c * chunk : (c + 1) * chunk] = total.astype(jnp.bfloat16)


def expert_kernel(tile, halves, x, w_gate_up, w_out, out, acc):
    half = pl.program_id(1)
    rows = x.shape[2]
    chunk = x.shape[3]
    for t in range(rows // tile):
        at = slice(t * tile, (t + 1) * tile)
        arrived = jnp.concatenate([x[c, 0, at, :] for c in range(CHUNKS)], axis=1)
        contract = (((1,), (1,)), ((), ()))
        gate = lax.dot_general(arrived, w_gate_up[0, 0], contract, preferred_element_type=jnp.float32)
        up = lax.dot_general(arrived, w_gate_up[0, 1], contract, preferred_element_type=jnp.float32)
        hidden = (gate / (1.0 + jnp.exp(-gate)) * up).astype(jnp.bfloat16)
        made = jnp.dot(hidden, w_out[0], preferred_element_type=jnp.float32)

        @pl.when(half == 0)
        def _():
            acc[at, :] = made

        @pl.when(half == halves - 1)
        def _():
            total = acc[at, :] + made
            for c in range(CHUNKS):
                out[c, 0, at, :] = total[:, c * chunk : (c + 1) * chunk].astype(jnp.bfloat16)


def moe(tokens, route_weight, slots, w_in, w_out):
    n_group, n_inner = lax.axis_size("group"), lax.axis_size("inner")
    batches, tok_count, width = tokens.shape
    slot_dev = w_in.shape[0]
    depth = 4 if n_inner % 4 == 0 else 1
    n_width = n_inner // depth
    planes = n_group * n_width
    box_rows = batches * depth * MOST
    rows = planes * slot_dev * box_rows
    count = depth * batches * tok_count
    chunk = width // CHUNKS
    order = jnp.arange(tok_count * TOPK, dtype=jnp.int32)
    same = (slots[:, :, None] == slots[:, None, :]) & (order[None, None, :] < order[None, :, None])
    position = jnp.sum(same.astype(jnp.int32), axis=2)
    code = (slots * MOST + position).reshape(batches, tok_count, TOPK)
    meta = jnp.stack([code.astype(jnp.float32), route_weight])
    lines = [[p * n_width + y for p in range(depth)] for y in range(n_width)]
    meta = lax.all_gather(meta, "inner", axis_index_groups=lines)
    code = meta[:, 0].astype(jnp.int32)
    target, position = code // MOST, code % MOST
    device, local_slot = target // slot_dev, target % slot_dev
    dev_group, dev_inner = device // n_inner, device % n_inner
    plane = dev_group * n_width + dev_inner % n_width
    source = jnp.arange(depth, dtype=jnp.int32)[:, None, None, None]
    batch = jnp.arange(batches, dtype=jnp.int32)[None, :, None, None]
    row = (plane * slot_dev + local_slot) * box_rows + (source * batches + batch) * MOST + position
    row = jnp.where(dev_inner // n_width == lax.axis_index("inner") // n_width, row, -1)
    row = jnp.pad(row.reshape(count, TOPK), ((0, 0), (0, 2)), constant_values=-1)
    weight = jnp.pad(meta[:, 1].reshape(count, TOPK), ((0, 0), (0, 2)))
    vmem, hbm = pl.BlockSpec(memory_space=pltpu.VMEM), pl.BlockSpec(memory_space=pl.ANY)
    sem = pltpu.SemaphoreType.DMA
    arrived = pl.pallas_call(
        partial(dispatch_kernel, depth, n_inner, planes),
        out_shape=jax.ShapeDtypeStruct((CHUNKS, slot_dev, planes, box_rows, chunk), jnp.bfloat16),
        in_specs=[vmem, vmem],
        out_specs=hbm,
        scratch_shapes=[
            pltpu.VMEM((CHUNKS, depth, batches * tok_count, chunk), jnp.bfloat16),
            pltpu.VMEM((rows, count), jnp.bfloat16),
            pltpu.VMEM((CHUNKS, planes, slot_dev, box_rows, chunk), jnp.bfloat16),
            sem((CHUNKS, depth)),
            sem((CHUNKS, depth)),
            sem((CHUNKS, planes)),
            sem((CHUNKS, planes)),
            sem((CHUNKS,)),
        ],
        compiler_params=pltpu.CompilerParams(
            collective_id=1, has_side_effects=True, vmem_limit_bytes=40 * 2**20
        ),
        name="dispatch",
    )(tokens.reshape(batches * tok_count, width), row.T)
    halves = 2
    slot_rows = planes * box_rows
    tile = 384 if slot_rows % 384 == 0 else slot_rows
    mode = {} if slot_rows <= 384 else {"pipeline_mode": pl.Buffered(1)}
    part_ff = FF // halves
    act = pl.BlockSpec((CHUNKS, 1, slot_rows, chunk), lambda s, h: (0, s, 0, 0), **mode)
    served = pl.pallas_call(
        partial(expert_kernel, tile, halves),
        grid=(slot_dev, halves),
        out_shape=jax.ShapeDtypeStruct((CHUNKS, slot_dev, slot_rows, chunk), jnp.bfloat16),
        in_specs=[
            act,
            pl.BlockSpec((1, 2, part_ff, width), lambda s, h: (s, 0, h, 0)),
            pl.BlockSpec((1, part_ff, width), lambda s, h: (s, h, 0)),
        ],
        out_specs=act,
        scratch_shapes=[pltpu.VMEM((slot_rows, width), jnp.float32)],
        compiler_params=pltpu.CompilerParams(
            vmem_limit_bytes=60 * 2**20, dimension_semantics=("arbitrary", "arbitrary")
        ),
        cost_estimate=pl.CostEstimate(
            flops=6 * slot_dev * slot_rows * FF * width,
            bytes_accessed=6 * slot_dev * FF * width,
            transcendentals=0,
        ),
        name="experts",
    )(
        arrived.reshape(CHUNKS, slot_dev, slot_rows, chunk),
        w_in.reshape(slot_dev, 2, FF, width),
        w_out,
    )
    combined = pl.pallas_call(
        partial(return_kernel, depth, n_inner, planes),
        out_shape=jax.ShapeDtypeStruct((batches * tok_count, width), jnp.bfloat16),
        in_specs=[hbm, vmem, vmem],
        out_specs=vmem,
        scratch_shapes=[
            pltpu.VMEM((CHUNKS, planes, slot_dev, box_rows, chunk), jnp.bfloat16),
            pltpu.VMEM((count, rows), jnp.bfloat16),
            pltpu.VMEM((count, rows), jnp.bfloat16),
            pltpu.VMEM((depth, batches * tok_count, chunk), jnp.float32),
            pltpu.VMEM((CHUNKS, depth, batches * tok_count, chunk), jnp.bfloat16),
            pltpu.VMEM((CHUNKS, batches * tok_count, chunk), jnp.float32),
            pltpu.VMEM((CHUNKS, depth, batches * tok_count, chunk), jnp.bfloat16),
            sem((CHUNKS, planes)),
            sem((CHUNKS, planes)),
            sem((CHUNKS,)),
            sem((CHUNKS, depth)),
            sem((CHUNKS, depth)),
        ],
        compiler_params=pltpu.CompilerParams(
            collective_id=2, has_side_effects=True, vmem_limit_bytes=48 * 2**20
        ),
        name="give_back",
    )(served.reshape(CHUNKS, slot_dev, planes, box_rows, chunk), row, weight)
    return combined.reshape(batches, tok_count, width)


def local(
    tokens,
    route_weight,
    routes,
    replica,
    old_place,
    new_src,
    w_in,
    w_out,
    queries,
    latent_cache,
    block_req,
    block_len,
):
    slot_index = jnp.arange(old_place.shape[0], dtype=jnp.int32)
    keys = jnp.stack([replica_keys(old_place), replica_keys(table_lookup(new_src, old_place))])
    weight_slot = jnp.stack([slot_index, new_src])
    route_key = (routes * 2 + replica).reshape(2, -1)
    slots = jnp.sum(
        jnp.where(route_key[:, :, None] == keys[:, None, :], weight_slot[:, None, :], 0), axis=2
    )
    moe_out = moe(tokens, route_weight, slots, w_in, w_out)
    attend = jax.vmap(partial(block_attention, latent=LAT))
    req_max, req_total, req_out = attend(queries, latent_cache, block_req, block_len)
    attention = join_attention(req_max, req_total, req_out, "inner")
    return (moe_out, attention)


def solution(mesh):
    in_specs = (
        P(None, ("group", "inner"), None),
        P(None, ("group", "inner"), None),
        P(None, ("group", "inner"), None),
        P(None, ("group", "inner"), None),
        P(),
        P(),
        P(("group", "inner"), None, None),
        P(("group", "inner"), None, None),
        P(None, "group", None, None),
        P(None, ("group", "inner"), None, None),
        P(None, ("group", "inner")),
        P(None, ("group", "inner")),
    )
    out_specs = (P(None, ("group", "inner"), None), P(None, "group", None, None))
    return jax.shard_map(local, mesh=mesh, in_specs=in_specs, out_specs=out_specs, check_vma=False)
```

time: 473 us -> 297 us (0.63); the launches traced: 466 us -> 296 us
  Pallas kernels: 0 us -> 209 us
  waiting for transfers between devices: 95 us -> 0.01 us
  matrix products: 104 us -> 10.8 us
  blocking collectives: 121 us -> 45.7 us
  local copies, waits for them, and re-layouts: 77.2 us -> 8.03 us
  other arithmetic: 34.6 us -> 5.08 us
  between operations: 14.5 us -> 0.97 us
    pallas_call x0 -> x3, Pallas kernels: none -> 209 us  [the longest x1 87.6 us: moe(): pl.pallas_call(partial(return_kernel, depth, n_inner, planes), out_shape=...]
    all_to_all x4 -> x2, waiting for transfers between devices: 95 us -> 0.01 us  [the longest x1 0.01 us: join_attention(): stats = lax.all_to_all(stats, axis, split_axis=0, concat_axis=0, tiled=True)]
    dot_general x8 -> x0, matrix products: 92.7 us -> none  [the longest x2 49.3 us: expert_block(): jnp.einsum('nsmd,sfd->nsmf', arrived, w_in, preferred_element_type=jnp.fl...]
    all_gather x2, blocking collectives: 121 us -> 45.7 us  [the longest x1 32.1 us: join_attention(): whole = lax.all_gather(own, axis, axis=0, tiled=True)]
    another operation x8 -> x2, local copies, waits for them, and re-layouts: 23.5 us -> 0.14 us  [join_attention(): jnp.stack([req_max.reshape(n, share), req_total.reshape(n, share)], axis=1)]
    add x16 -> x2, other arithmetic: 14.1 us -> 0.01 us  [the longest x1 0.01 us: local(): route_key = (routes * 2 + replica).reshape(2, -1)]
    all_to_all x2 -> x0, local copies, waits for them, and re-layouts: 12.3 us -> none  [moe_batch(): lax.all_to_all(served, ('group', 'inner'), split_axis=0, concat_axis=0, t...]
    reshape x2 -> x0, local copies, waits for them, and re-layouts: 11.3 us -> none  [moe_batch(): flat_rows = returned.reshape(slot_count * MOST, feat_width)]
  transfers between devices with their start and end apart: 5 -> 2, of which waited for: 3 -> 0; matrix products, arithmetic and copies ran while one was open for 38% -> 3% of each run, Pallas kernels for 0% -> 70%
where the time goes in v1:
time: 297 us; the launch traced here: 296 us
  Pallas kernels  209 us (70%)
  blocking collectives  45.7 us (15%)
  starting transfers between devices  17.2 us (6%)
  matrix products  10.8 us (4%)
  local copies, waits for them, and re-layouts  8.03 us (3%)
  other arithmetic  5.08 us (2%)
    pallas_call x1, Pallas kernels, moe(): pl.pallas_call(partial(return_kernel, depth, n_inner, planes), out_shape=...  87.6 us
    pallas_call x1, Pallas kernels, moe(): pl.pallas_call(partial(dispatch_kernel, depth, n_inner, planes), out_shap...  82.8 us
    pallas_call x1, Pallas kernels, moe(): pl.pallas_call(partial(expert_kernel, tile, halves), grid=(slot_dev, halv...  38.2 us
    all_gather x1, blocking collectives, join_attention(): whole = lax.all_gather(own, axis, axis=0, tiled=True)  32.1 us
    all_gather x1, blocking collectives, moe(): meta = lax.all_gather(meta, 'inner', axis_index_groups=lines)  13.6 us
    all_to_all x1, starting transfers between devices, join_attention(): parts = lax.all_to_all(parts, axis, split_axis=0, concat_axis=0, tiled=True)  9.93 us
    all_to_all x1, starting transfers between devices, join_attention(): stats = lax.all_to_all(stats, axis, split_axis=0, concat_axis=0, tiled=True)  7.28 us
  transfers between devices with their start and end apart: 2, of which 0 were waited for; matrix products, arithmetic and copies ran while one was open for 3% of the time, Pallas kernels for 70%

profile of v1, /device:TPU:0, one launch (start us, length us, event | category | flops | bytes accessed | tf_op | source)
XLA Modules:
  0.0 296.4 jit_solution(4816982980424916144)
XLA Ops:
  0.6 0.0 copy-start.2
  0.7 1.3 reshape.179
  2.0 0.7 iota_compare_fusion.4
  2.7 1.0 convolution_convert_fusion
  3.7 0.4 reshape.185
  4.2 0.8 iota_compare_fusion.3
  4.9 0.1 copy.47
  5.0 4.2 %fusion.36 = (f32[2,12,16]{2,1,0:T(8,128)S(1)}, f32[2,12,16,256]{3,2,1,0:T(8,128)S(1)}) fusion(bf16[2,12,16,576]{3,2,1,0:T(8,128)(2,1)S(1)} %reshape.185, bf16[2,12,256,576]{2,3,1,0:T(8,128)(2,1)} %param.21, pred[2,12,256]{2,1,0:T(8,128)(4,1)S(1)} %iota_compare_fusion.3), kind=kOutput, calls=%fused_computation.92 | convolution fusion | flops 113540736 | bytes 7921152 | tf_op jit(solution)/shard_map/vmap(chk,cpk->chp)/dot_general | solution.py:34
  9.2 0.1 select_reduce_fusion.2
  9.3 0.1 select_reduce_fusion.1
  9.4 0.1 stack_reshape.6
  9.5 0.2 fusion.4
  9.7 0.1 fusion.28
  9.9 0.1 stack_reshape.7
  10.0 0.6 pad_maximum_fusion.1
  10.6 7.3 %all-to-all-start.1 = ((f32[8,2,32]{2,1,0:T(2,128)}), f32[8,2,32]{2,1,0:T(2,128)S(1)}, u32[]{:S(2)}, u32[]{:S(2)}) async-start(f32[8,2,32]{2,1,0:T(2,128)} %pad_maximum_fusion.1), calls=%async_computation.1 | async-start | bytes 16384 | tf_op jit(solution)/shard_map/all_to_all | solution.py:60
  17.9 0.2 convert_reduce_fusion.2
  18.1 0.2 convert_reduce_fusion.1
  18.3 0.1 copy.40
  18.4 0.1 eq.94
  18.6 0.3 select_reduce_fusion
  18.9 0.4 convert_reduce_fusion
  19.4 0.1 convert_element_type.50
  19.5 0.1 copy.41
  19.6 13.6 %all-gather = f32[8,2,64,6]{2,1,3,0:T(2,128)S(1)} all-gather(f32[2,2,64,6]{2,1,3,0:T(2,128)S(1)} %pad_maximum_fusion), channel_id=2, replica_groups={{0,2,4,6},{1,3,5,7},{8,10,12,14},{9,11,13,15},{16,18,20,22},{17,19,21,2..., dimensions={0}, use_global_device_ids=true | all-gather | bytes 30720 | tf_op jit(solution)/shard_map/all_gather | solution.py:257
  33.3 0.2 copy.56
  33.4 0.1 convert_divide_fusion
  33.6 0.1 sign_compare_fusion.3
  33.7 4.5 %fusion = f32[2,12,16,512]{3,2,1,0:T(8,128)S(1)} fusion(bf16[2,12,256,576]{2,3,1,0:T(8,128)(2,1)} %param.21, f32[2,12,16,256]{3,2,1,0:T(8,128)S(1)} %get-tuple-element.15, f32[2,12,16]{2,1,0:T(8,128)S(1)} %select_reduce_fusion.1, pred[2,12,256]{2,1,0:T(8,128)(4,1)S(1)} %iota_compare_fusion.3), kind=kOutput, calls=%fused_computation.1 | convolution fusion | flops 100958208 | bytes 7478784 | tf_op jit(solution)/shard_map/vmap(chp,cpl->chl)/dot_general | solution.py:45
  38.2 0.1 add_multiply_fusion
  38.3 0.1 add.122
  38.3 0.1 add.123
  38.4 0.9 convolution_convert_fusion.1
  39.4 0.9 fusion.14
  40.3 0.1 copy.43.row
  40.4 0.8 copy.50
  41.2 82.8 %dispatch.1 = bf16[4,4,8,48,512]{4,3,2,1,0:T(8,128)(2,1)S(1)} custom-call(bf16[128,2048]{1,0:T(8,128)(2,1)S(1)} %bitcast.56, s32[8,512]{1,0:T(8,128)S(1)} %copy.43.row), custom_call_target="tpu_custom_call" | custom-call | tf_op jit(solution)/shard_map/dispatch/pallas_call | solution.py:271
  124.0 2.7 copy-done
  126.6 0.0 all-to-all-done.1
  126.6 9.9 %all-to-all-start = ((bf16[8,32,512]{2,1,0:T(8,128)(2,1)}), bf16[8,32,512]{2,1,0:T(8,128)(2,1)S(1)}, u32[]{:S(2)}, u32[]{:S(2)}) async-start(bf16[8,32,512]{2,1,0:T(8,128)(2,1)} %bitcast.17), calls=%async_computation | async-start | bytes 524288 | tf_op jit(solution)/shard_map/all_to_all | solution.py:61
  136.6 38.2 %experts.1 = bf16[4,4,384,512]{3,2,1,0:T(8,128)(2,1)} custom-call(bf16[4,4,384,512]{3,2,1,0:T(8,128)(2,1)} %bitcast.54, bf16[4,2,1408,2048]{3,2,1,0:T(8,128)(2,1)} %bitcast.68, bf16[4,1408,2048]{2,1,0:T(8,128)(2,1)} %w_out.1), custom_call_target="tpu_custom_call" | custom-call | flops 26575110144 | bytes 69206016 | tf_op jit(solution)/shard_map/experts/pallas_call | solution.py:297
  174.7 0.1 copy.57
  174.9 87.6 %give_back.1 = bf16[128,2048]{1,0:T(8,128)(2,1)S(1)} custom-call(bf16[4,4,8,48,512]{4,3,2,1,0:T(8,128)(2,1)} %bitcast.57, s32[512,8]{1,0:T(8,128)S(1)} %get-tuple-element.6.row, f32[512,8]{1,0:T(8,128)S(1)} %pad.9.weight), custom_call_target="tpu_custom_call" | custom-call | tf_op jit(solution)/shard_map/give_back/pallas_call | solution.py:322
  262.6 0.1 multiply_reduce_fusion
  262.8 0.1 divide_convert_fusion
  262.8 32.1 %all_gather.11 = bf16[256,512]{1,0:T(8,128)(2,1)S(1)} all-gather(bf16[32,512]{1,0:T(8,128)(2,1)S(1)} %divide_convert_fusion), channel_id=1, replica_groups=mesh['group'=4,'inner'=8] {'inner'}, dimensions={0}, use_global_device_ids=true | all-gather | bytes 294912 | tf_op jit(solution)/shard_map/all_gather | solution.py:67
  294.9 0.8 copy.64
  295.7 0.7 copy.65
  (30 shorter events, 0.3 us)
Async XLA Ops:
  0.6 9.1 %copy-start.2 = (s32[2,12]{1,0:T(2,128)S(1)}, s32[2,12]{1,0:T(2,128)}, u32[]{:S(2)}) copy-start(s32[2,12]{1,0:T(2,128)} %param.22) | copy-start | bytes 292
  0.6 17.3 %copy-start.7 = (s32[128]{0:T(128)S(1)}, s32[128]{0:T(128)}, u32[]{:S(2)}) copy-start(s32[128]{0:T(128)} %param.17) | copy-start | bytes 1540
  0.7 17.3 %copy-start.6 = (s32[128]{0:T(128)S(1)}, s32[128]{0:T(128)}, u32[]{:S(2)}) copy-start(s32[128]{0:T(128)} %param.16) | copy-start | bytes 1540
  0.7 17.6 %copy-start.3 = (s32[2,64,6]{1,0,2:T(2,128)S(1)}, s32[2,64,6]{1,0,2:T(2,128)}, u32[]{:S(2)}) copy-start(s32[2,64,6]{1,0,2:T(2,128)} %param.15) | copy-start | bytes 9220
  0.7 17.6 %copy-start.4 = (s32[2,64,6]{1,0,2:T(2,128)S(1)}, s32[2,64,6]{1,0,2:T(2,128)}, u32[]{:S(2)}) copy-start(s32[2,64,6]{1,0,2:T(2,128)} %param.14) | copy-start | bytes 9220
  0.7 18.9 %copy-start.5 = (f32[2,64,6]{1,0,2:T(2,128)S(1)}, f32[2,64,6]{1,0,2:T(2,128)}, u32[]{:S(2)}) copy-start(f32[2,64,6]{1,0,2:T(2,128)} %param.13) | copy-start | bytes 9220
  9.2 32.0 %copy-start.1 = (bf16[2,64,2048]{2,1,0:T(8,128)(2,1)S(1)}, bf16[2,64,2048]{2,1,0:T(8,128)(2,1)}, u32[]{:S(2)}) copy-start(bf16[2,64,2048]{2,1,0:T(8,128)(2,1)} %param.12) | copy-start | bytes 1572868
  10.6 116.1 %all-to-all-start.1 = ((f32[8,2,32]{2,1,0:T(2,128)}), f32[8,2,32]{2,1,0:T(2,128)S(1)}, u32[]{:S(2)}, u32[]{:S(2)}) async-start(f32[8,2,32]{2,1,0:T(2,128)} %pad_maximum_fusion.1), calls=%async_computation.1 | async-start | bytes 16384 | tf_op jit(solution)/shard_map/all_to_all | solution.py:60
  124.0 2.7 copy-start
  126.6 136.0 %all-to-all-start = ((bf16[8,32,512]{2,1,0:T(8,128)(2,1)}), bf16[8,32,512]{2,1,0:T(8,128)(2,1)S(1)}, u32[]{:S(2)}, u32[]{:S(2)}) async-start(bf16[8,32,512]{2,1,0:T(8,128)(2,1)} %bitcast.17), calls=%async_computation | async-start | bytes 524288 | tf_op jit(solution)/shard_map/all_to_all | solution.py:61

commit v2 on v1

--- a/solution.py
+++ b/solution.py
@@ -51,21 +51,12 @@
     return (req_max, req_total, req_out)
 
 
-def join_attention(req_max, req_total, req_out, axis):
-    n = lax.axis_size(axis)
+def split_attention(req_max, req_total, req_out, n):
     batches, requests, heads, latent = req_out.shape
     share = batches * requests * heads // n
-    stats = jnp.stack([req_max.reshape(n, share), req_total.reshape(n, share)], axis=1)
-    parts = req_out.astype(jnp.bfloat16).reshape(n, share, latent)
-    stats = lax.all_to_all(stats, axis, split_axis=0, concat_axis=0, tiled=True)
-    parts = lax.all_to_all(parts, axis, split_axis=0, concat_axis=0, tiled=True)
-    joint = jnp.max(stats[:, 0], axis=0)
-    scale = jnp.exp(stats[:, 0] - joint[None])
-    total = jnp.sum(stats[:, 1] * scale, axis=0)
-    summed = jnp.sum(parts.astype(jnp.float32) * scale[..., None], axis=0)
-    own = (summed / total[:, None]).astype(jnp.bfloat16)
-    whole = lax.all_gather(own, axis, axis=0, tiled=True)
-    return whole.reshape(batches, requests, heads, latent)
+    stats = jnp.stack([req_max.reshape(n, share), req_total.reshape(n, share)], axis=2)
+    stats = jnp.pad(stats, ((0, 0), (0, 0), (0, 126)))
+    return stats, req_out.astype(jnp.bfloat16).reshape(n, share, latent)
 
 
 def replica_keys(expert_of_slot):
@@ -102,13 +93,27 @@
     )
 
 
-def dispatch_kernel(depth, n_inner, planes, tok, row, out, gat, tab, box, zs, zr, ps, pr, ls):
+def dispatch_kernel(
+    depth, n_inner, planes, tok, rid, rw, stats, parts, out, row_out, rw_out, whole,
+    gat, tab, box, rowg, rwg, got_stats, got_parts, joined,
+    zs, zr, ps, pr, ls, ms, mr, ws, wr, ss, sr, qs, qr, js, jr, jl,
+):
     z, me, line, plane = places(depth, n_inner)
     line_to = [lax.rem(z + k, depth) for k in range(1, depth)]
     plane_to = [lax.rem(me + k, planes) for k in range(1, planes)]
-    greet([line(p) for p in line_to] + [plane(p) for p in plane_to])
+    g, i = lax.axis_index("group"), lax.axis_index("inner")
+    inner_to = [lax.rem(i + k, n_inner) for k in range(1, n_inner)]
+    greet(
+        [line(p) for p in line_to] + [plane(p) for p in plane_to] + [(g, p) for p in inner_to]
+    )
     chunk = gat.shape[3]
     per_box = tab.shape[0] // planes
+    metas, shares = [], []
+    for k, p in enumerate(line_to):
+        metas.append(remote(rid, rowg.at[z], ms.at[k], mr.at[k], line(p)))
+        metas.append(remote(rw, rwg.at[z], ws.at[k], wr.at[k], line(p)))
+    for copy in metas:
+        copy.start()
     flights = []
     for c in range(CHUNKS):
         flight = []
@@ -119,16 +124,34 @@
             copy.start()
             flight.append(copy)
         flights.append(flight)
+    for k, p in enumerate(inner_to):
+        shares.append(remote(stats.at[p], got_stats.at[i], ss.at[k], sr.at[k], (g, p)))
+        shares.append(remote(parts.at[p], got_parts.at[i], qs.at[k], qr.at[k], (g, p)))
+    for copy in shares:
+        copy.start()
     for c in range(CHUNKS):
         gat[c, z] = tok[:, c * chunk : (c + 1) * chunk]
+    rowg[z] = rid[...]
+    rwg[z] = rw[...]
+    got_stats[i] = stats[i]
+    got_parts[i] = parts[i]
+    for copy in metas:
+        copy.wait()
+    row_out[...] = rowg[...]
+    rw_out[...] = rwg[...]
     step = 256
+    per_source = tok.shape[0]
 
     def fill(t, carry):
-        rows = lax.broadcasted_iota(jnp.int32, (step, tab.shape[1]), 0) + t * step
-        total = jnp.zeros((step, tab.shape[1]), jnp.float32)
-        for k in range(TOPK):
-            total = total + jnp.where(rows == row[k : k + 1, :], 1.0, 0.0)
-        tab[pl.ds(pl.multiple_of(t * step, step), step), :] = total.astype(jnp.bfloat16)
+        first = t * step + z * tab.shape[0]
+        rows = lax.broadcasted_iota(jnp.int32, (step, per_source), 0) + first
+        for s in range(depth):
+            total = jnp.zeros((step, per_source), jnp.float32)
+            for k in range(TOPK):
+                total = total + jnp.where(rows == rowg[s, k : k + 1, :], 1.0, 0.0)
+            tab[
+                pl.ds(pl.multiple_of(t * step, step), step), s * per_source : (s + 1) * per_source
+            ] = total.astype(jnp.bfloat16)
         return carry
 
     lax.fori_loop(0, tab.shape[0] // step, fill, 0)
@@ -152,6 +175,26 @@
         own = pltpu.make_async_copy(box.at[c, me], out.at[c, :, me], ls.at[c])
         own.start()
         sends.append(own)
+        if c == 0:
+            for copy in shares:
+                copy.wait()
+            joint = got_stats[0, :, 0:1]
+            for p in range(1, n_inner):
+                joint = jnp.maximum(joint, got_stats[p, :, 0:1])
+            total = jnp.zeros_like(joint)
+            summed = jnp.zeros(joined.shape, jnp.float32)
+            for p in range(n_inner):
+                scale = jnp.exp(got_stats[p, :, 0:1] - joint)
+                total = total + got_stats[p, :, 1:2] * scale
+                summed = summed + got_parts[p].astype(jnp.float32) * scale
+            joined[...] = (summed / total).astype(jnp.bfloat16)
+            for k, p in enumerate(inner_to):
+                copy = remote(joined, whole.at[i], js.at[k], jr.at[k], (g, p))
+                copy.start()
+                sends.append(copy)
+            kept = pltpu.make_async_copy(joined, whole.at[i], jl)
+            kept.start()
+            sends.append(kept)
     for flight in flights:
         for copy in flight:
             copy.wait_send()
@@ -237,7 +280,7 @@
                 out[c, 0, at, :] = total[:, c * chunk : (c + 1) * chunk].astype(jnp.bfloat16)
 
 
-def moe(tokens, route_weight, slots, w_in, w_out):
+def layer(tokens, route_weight, slots, w_in, w_out, stats, parts):
     n_group, n_inner = lax.axis_size("group"), lax.axis_size("inner")
     batches, tok_count, width = tokens.shape
     slot_dev = w_in.shape[0]
@@ -251,43 +294,55 @@
     order = jnp.arange(tok_count * TOPK, dtype=jnp.int32)
     same = (slots[:, :, None] == slots[:, None, :]) & (order[None, None, :] < order[None, :, None])
     position = jnp.sum(same.astype(jnp.int32), axis=2)
-    code = (slots * MOST + position).reshape(batches, tok_count, TOPK)
-    meta = jnp.stack([code.astype(jnp.float32), route_weight])
-    lines = [[p * n_width + y for p in range(depth)] for y in range(n_width)]
-    meta = lax.all_gather(meta, "inner", axis_index_groups=lines)
-    code = meta[:, 0].astype(jnp.int32)
-    target, position = code // MOST, code % MOST
-    device, local_slot = target // slot_dev, target % slot_dev
+    device, local_slot = slots // slot_dev, slots % slot_dev
     dev_group, dev_inner = device // n_inner, device % n_inner
     plane = dev_group * n_width + dev_inner % n_width
-    source = jnp.arange(depth, dtype=jnp.int32)[:, None, None, None]
-    batch = jnp.arange(batches, dtype=jnp.int32)[None, :, None, None]
+    source = lax.axis_index("inner") // n_width
+    batch = jnp.arange(batches, dtype=jnp.int32)[:, None]
     row = (plane * slot_dev + local_slot) * box_rows + (source * batches + batch) * MOST + position
-    row = jnp.where(dev_inner // n_width == lax.axis_index("inner") // n_width, row, -1)
-    row = jnp.pad(row.reshape(count, TOPK), ((0, 0), (0, 2)), constant_values=-1)
-    weight = jnp.pad(meta[:, 1].reshape(count, TOPK), ((0, 0), (0, 2)))
+    row = row + (dev_inner // n_width) * rows
+    row = row.reshape(batches * tok_count, TOPK).T
+    row = jnp.pad(row, ((0, 2), (0, 0)), constant_values=-1)
+    weight = jnp.pad(route_weight.reshape(batches * tok_count, TOPK).T, ((0, 2), (0, 0)))
     vmem, hbm = pl.BlockSpec(memory_space=pltpu.VMEM), pl.BlockSpec(memory_space=pl.ANY)
     sem = pltpu.SemaphoreType.DMA
-    arrived = pl.pallas_call(
+    per_source = batches * tok_count
+    arrived, row, weight, attention = pl.pallas_call(
         partial(dispatch_kernel, depth, n_inner, planes),
-        out_shape=jax.ShapeDtypeStruct((CHUNKS, slot_dev, planes, box_rows, chunk), jnp.bfloat16),
-        in_specs=[vmem, vmem],
-        out_specs=hbm,
+        out_shape=(
+            jax.ShapeDtypeStruct((CHUNKS, slot_dev, planes, box_rows, chunk), jnp.bfloat16),
+            jax.ShapeDtypeStruct((depth, 8, per_source), jnp.int32),
+            jax.ShapeDtypeStruct((depth, 8, per_source), jnp.float32),
+            jax.ShapeDtypeStruct(parts.shape, jnp.bfloat16),
+        ),
+        in_specs=[vmem] * 5,
+        out_specs=(hbm, vmem, vmem, hbm),
         scratch_shapes=[
             pltpu.VMEM((CHUNKS, depth, batches * tok_count, chunk), jnp.bfloat16),
             pltpu.VMEM((rows, count), jnp.bfloat16),
             pltpu.VMEM((CHUNKS, planes, slot_dev, box_rows, chunk), jnp.bfloat16),
+            pltpu.VMEM((depth, 8, per_source), jnp.int32),
+            pltpu.VMEM((depth, 8, per_source), jnp.float32),
+            pltpu.VMEM(stats.shape, jnp.float32),
+            pltpu.VMEM(parts.shape, jnp.bfloat16),
+            pltpu.VMEM(parts.shape[1:], jnp.bfloat16),
             sem((CHUNKS, depth)),
             sem((CHUNKS, depth)),
             sem((CHUNKS, planes)),
             sem((CHUNKS, planes)),
             sem((CHUNKS,)),
-        ],
+        ]
+        + [sem((depth,))] * 4
+        + [sem((n_inner,))] * 6
+        + [sem],
         compiler_params=pltpu.CompilerParams(
             collective_id=1, has_side_effects=True, vmem_limit_bytes=40 * 2**20
         ),
         name="dispatch",
-    )(tokens.reshape(batches * tok_count, width), row.T)
+    )(tokens.reshape(batches * tok_count, width), row, weight, stats, parts)
+    first = (lax.axis_index("inner") // n_width) * rows
+    row = row.transpose(0, 2, 1).reshape(count, 8) - first
+    weight = weight.transpose(0, 2, 1).reshape(count, 8)
     halves = 2
     slot_rows = planes * box_rows
     tile = 384 if slot_rows % 384 == 0 else slot_rows
@@ -343,7 +398,7 @@
         ),
         name="give_back",
     )(served.reshape(CHUNKS, slot_dev, planes, box_rows, chunk), row, weight)
-    return combined.reshape(batches, tok_count, width)
+    return combined.reshape(batches, tok_count, width), attention
 
 
 def local(
@@ -367,10 +422,11 @@
     slots = jnp.sum(
         jnp.where(route_key[:, :, None] == keys[:, None, :], weight_slot[:, None, :], 0), axis=2
     )
-    moe_out = moe(tokens, route_weight, slots, w_in, w_out)
     attend = jax.vmap(partial(block_attention, latent=LAT))
-    req_max, req_total, req_out = attend(queries, latent_cache, block_req, block_len)
-    attention = join_attention(req_max, req_total, req_out, "inner")
+    partial_attention = attend(queries, latent_cache, block_req, block_len)
+    stats, parts = split_attention(*partial_attention, lax.axis_size("inner"))
+    moe_out, attention = layer(tokens, route_weight, slots, w_in, w_out, stats, parts)
+    attention = attention.reshape(queries.shape[:3] + (LAT,))
     return (moe_out, attention)
 
 

time: 297 us -> 267 us (0.90)
  blocking collectives: 45.7 us -> 0 us
  Pallas kernels: 209 us -> 241 us
  starting transfers between devices: 17.2 us -> 0 us
    all_gather x2 -> x0, blocking collectives: 45.7 us -> none  [the longest x1 32.1 us: join_attention(): whole = lax.all_gather(own, axis, axis=0, tiled=True)]
    pallas_call x3, Pallas kernels: 209 us -> 241 us  [the longest x1 118 us: layer(): pl.pallas_call(partial(dispatch_kernel, depth, n_inner, planes), out_shap...]
    all_to_all x2 -> x0, starting transfers between devices: 17.2 us -> none  [the longest x1 9.93 us: join_attention(): parts = lax.all_to_all(parts, axis, split_axis=0, concat_axis=0, tiled=True)]
  transfers between devices with their start and end apart: 2 -> 0, of which waited for: 0 -> 0; matrix products, arithmetic and copies ran while one was open for 3% -> 0% of each run, Pallas kernels for 70% -> 0%
where the time goes in v2:
time: 267 us
  Pallas kernels  241 us (90%)
  matrix products  10.8 us (4%)
  local copies, waits for them, and re-layouts  8.16 us (3%)
  other arithmetic  5.88 us (2%)
    pallas_call x1, Pallas kernels, layer(): pl.pallas_call(partial(dispatch_kernel, depth, n_inner, planes), out_shap...  118 us
    pallas_call x1, Pallas kernels, layer(): pl.pallas_call(partial(return_kernel, depth, n_inner, planes), out_shape=...  85.4 us
    pallas_call x1, Pallas kernels, layer(): pl.pallas_call(partial(expert_kernel, tile, halves), grid=(slot_dev, halv...  38.1 us

profile of v2, /device:TPU:0, one launch (start us, length us, event | category | flops | bytes accessed | tf_op | source)
XLA Modules:
  0.0 266.9 jit_solution(8745664306960390085)
XLA Ops:
  0.6 0.0 copy-start.2
  0.7 0.1 add.100
  0.7 0.1 add.101
  0.8 0.7 pad_add_fusion.1
  1.5 0.9 convert_reduce_fusion.2
  2.4 0.2 convert_reduce_fusion.1
  2.6 0.7 add_bitcast_fusion
  3.3 0.7 iota_compare_fusion.4
  3.9 0.1 copy.53
  4.0 0.8 reshape.105
  4.8 0.7 multiply_add_fusion
  5.5 0.8 iota_compare_fusion.3
  6.3 0.1 copy.47
  6.4 0.1 eq.86
  6.6 0.3 select_reduce_fusion
  6.9 0.1 reduce_sum.71
  7.0 0.1 copy.48
  7.1 0.1 iota_compare_fusion
  7.1 0.4 convert_reduce_fusion
  7.6 0.1 reduce_sum.73
  7.7 0.1 copy.52
  7.8 0.1 fusion.22
  7.8 1.2 reshape.106
  9.1 1.0 convolution_convert_fusion
  10.2 0.4 reshape.116
  10.6 4.2 %fusion.35 = (f32[2,12,16]{2,1,0:T(8,128)S(1)}, f32[2,12,16,256]{3,2,1,0:T(8,128)S(1)}) fusion(bf16[2,12,16,576]{3,2,1,0:T(8,128)(2,1)S(1)} %reshape.116, bf16[2,12,256,576]{2,3,1,0:T(8,128)(2,1)} %param.21, pred[2,12,256]{2,1,0:T(8,128)(4,1)S(1)} %iota_compare_fusion.3), kind=kOutput, calls=%fused_computation.76 | convolution fusion | flops 113540736 | bytes 7921152 | tf_op jit(solution)/shard_map/vmap(chk,cpk->chp)/dot_general | solution.py:34
  14.8 0.0 copy-start
  14.8 0.1 select_reduce_fusion.2
  14.9 0.1 stack_reshape.6
  15.0 0.1 select_reduce_fusion.1
  15.1 0.2 fusion.5
  15.3 0.0 copy-done.2
  15.3 0.1 fusion.13
  15.5 0.1 stack_reshape.7
  15.6 0.1 copy.56
  15.7 4.5 %fusion = f32[2,12,16,512]{3,2,1,0:T(8,128)S(1)} fusion(bf16[2,12,256,576]{2,3,1,0:T(8,128)(2,1)} %param.21, f32[2,12,16,256]{3,2,1,0:T(8,128)S(1)} %get-tuple-element.13, f32[2,12,16]{2,1,0:T(8,128)S(1)} %select_reduce_fusion.1, pred[2,12,256]{2,1,0:T(8,128)(4,1)S(1)} %iota_compare_fusion.3), kind=kOutput, calls=%fused_computation.1 | convolution fusion | flops 100958208 | bytes 7478784 | tf_op jit(solution)/shard_map/vmap(chp,cpl->chl)/dot_general | solution.py:45
  20.2 0.9 convolution_convert_fusion.1
  21.2 0.1 copy.59
  21.3 0.0 copy-done
  21.3 117.6 %dispatch.1 = (bf16[4,4,8,48,512]{4,3,2,1,0:T(8,128)(2,1)S(1)}, s32[4,8,128]{2,1,0:T(8,128)S(1)}, f32[4,8,128]{2,1,0:T(8,128)S(1)}, bf16[8,32,512]{2,1,0:T(8,128)(2,1)S(1)}) custom-call(bf16[128,2048]{1,0:T(8,128)(2,1)S(1)} %bitcast.37, s32[8,128]{1,0:T(8,128)S(1)} %pad.12.rid, f32[8,128]{1,0:T(8,128)S(1)} %pad.13.rw, f32[8,32,128]{2,1,0:T(8,128)S(1)} %pad.14.stats, ...), custom_call_target="tpu_custom_call" | custom-call | tf_op jit(solution)/shard_map/dispatch/pallas_call | solution.py:310
  138.9 0.0 copy-start.1
  138.9 2.7 copy-done.1
  141.6 38.1 %experts.1 = bf16[4,4,384,512]{3,2,1,0:T(8,128)(2,1)} custom-call(bf16[4,4,384,512]{3,2,1,0:T(8,128)(2,1)} %bitcast.40, bf16[4,2,1408,2048]{3,2,1,0:T(8,128)(2,1)} %bitcast.44, bf16[4,1408,2048]{2,1,0:T(8,128)(2,1)} %w_out.1), custom_call_target="tpu_custom_call" | custom-call | flops 26575110144 | bytes 69206016 | tf_op jit(solution)/shard_map/experts/pallas_call | solution.py:352
  179.7 0.1 copy.60
  179.9 0.1 copy.61
  180.0 85.4 %give_back.1 = bf16[128,2048]{1,0:T(8,128)(2,1)S(1)} custom-call(bf16[4,4,8,48,512]{4,3,2,1,0:T(8,128)(2,1)} %bitcast.41, s32[512,8]{1,0:T(8,128)S(1)} %bitcast.35, f32[512,8]{1,0:T(8,128)S(1)} %bitcast.36), custom_call_target="tpu_custom_call" | custom-call | tf_op jit(solution)/shard_map/give_back/pallas_call | solution.py:377
  265.4 0.8 copy.69
  266.2 0.7 copy.70
  (8 shorter events, 0.1 us)
Async XLA Ops:
  0.6 14.7 %copy-start.2 = (s32[2,12]{1,0:T(2,128)S(1)}, s32[2,12]{1,0:T(2,128)}, u32[]{:S(2)}) copy-start(s32[2,12]{1,0:T(2,128)} %param.22) | copy-start | bytes 292
  14.8 6.5 %copy-start = (bf16[2,64,2048]{2,1,0:T(8,128)(2,1)S(1)}, bf16[2,64,2048]{2,1,0:T(8,128)(2,1)}, u32[]{:S(2)}) copy-start(bf16[2,64,2048]{2,1,0:T(8,128)(2,1)} %param.12) | copy-start | bytes 1572868
  138.9 2.7 copy-start.1
